TPU v7x, 32 devices: a whole 2x2x4 slice. The times are simulated.
32 devices in a mesh: sub: 1, pts: 32 (over z, y, x, core).
Axes of the slice: x: 2, y: 2, z: 4, core: 2. Of those that a mesh axis runs over, the one named last changes fastest.
Arguments:
- cam_jac: float32 [2, 9, 4, 32768], P(None, None, None, ('sub', 'pts')), may hold values from -3 to 3
- point_jac: float32 [2, 3, 4, 32768], P(None, None, None, ('sub', 'pts')), may hold values from -3 to 3
- residuals: float32 [2, 4, 32768], P(None, None, ('sub', 'pts')), may hold values from -6 to 6
- obs_camera: int32 [4, 32768], P(None, ('sub', 'pts')), may hold values from 0 to 4095
- damping: float32 [1], P('sub'), may hold values from 0.01 to 0.1
Outputs:
- camera_step: float32 [9, 4096], P(None, ('sub', 'pts'))
- point_step: float32 [3, 32768], P(None, ('sub', 'pts'))
All inputs are finite; a program needn't handle non-finite values.
Results may differ from a plain program's by a relative error of at most 0.00022.
Values sent between devices are 32-bit elements; how exact they have to be, the bound alone decides.
A program may use at most 64 MiB of HBM per device.

v0:
```python
import jax
import jax.numpy as jnp
from jax import lax
from jax.sharding import PartitionSpec as P

NCAM = 4096
ITERS = 3
low_width = 16


def cofactor(matrix, row, col):
    kept_rows = [other for other in range(3) if other != row]
    kept_cols = [other for other in range(3) if other != col]
    sign = 1.0 if (row + col) % 2 == 0 else -1.0
    first = matrix[kept_rows[0], kept_cols[0]] * matrix[kept_rows[1], kept_cols[1]]
    second = matrix[kept_rows[0], kept_cols[1]] * matrix[kept_rows[1], kept_cols[0]]
    return sign * (first - second)


def point_inverse(point_jac, damp_value):
    gram = jnp.sum(point_jac[:, :, None] * point_jac[:, None, :], axis=(0, 3))
    gram = gram + damp_value * jnp.eye(3, dtype=jnp.float32)[:, :, None]
    determinant = (
        gram[0, 0] * cofactor(gram, 0, 0)
        + gram[0, 1] * cofactor(gram, 0, 1)
        + gram[0, 2] * cofactor(gram, 0, 2)
    )
    adjugate = jnp.stack(
        [jnp.stack([cofactor(gram, col, row) for col in range(3)]) for row in range(3)]
    )
    return adjugate / determinant[None, None]


def block_length():
    return 512


def hot_tables(camera_ids, high_width):
    upper_ids = camera_ids // low_width
    lower_ids = camera_ids % low_width
    length = camera_ids.shape[0]
    hot_high = (lax.broadcasted_iota(jnp.int32, (high_width, length), 0) == upper_ids[None]).astype(
        jnp.float32
    )
    hot_low = (lax.broadcasted_iota(jnp.int32, (low_width, length), 0) == lower_ids[None]).astype(
        jnp.float32
    )
    return (hot_high, hot_low)


def gather_cameras(camera_field, obs_camera):
    fields, cameras = camera_field.shape
    high_width = cameras // low_width
    lookup = (
        camera_field.reshape(fields, high_width, low_width)
        .transpose(0, 2, 1)
        .reshape(fields * low_width, high_width)
    )
    flat_ids = obs_camera.reshape(-1)
    count = flat_ids.shape[0]
    length = block_length()

    def one_block(camera_ids):
        hot_high, hot_low = hot_tables(camera_ids, high_width)
        picked = jnp.dot(lookup, hot_high, precision=lax.Precision.HIGHEST).reshape(
            fields, low_width, length
        )
        return jnp.sum(picked * hot_low[None], axis=1)

    pieces = lax.map(one_block, flat_ids.reshape(count // length, length))
    return pieces.transpose(1, 0, 2).reshape((fields,) + obs_camera.shape)


def scatter_cameras(values, obs_camera, cameras):
    fields = values.shape[0]
    high_width = cameras // low_width
    flat_ids = obs_camera.reshape(-1)
    count = flat_ids.shape[0]
    length = block_length()
    blocks = count // length
    value_blocks = values.reshape(fields, blocks, length).transpose(1, 0, 2)

    def add_block(running, item):
        camera_ids, block_values = item
        hot_high, hot_low = hot_tables(camera_ids, high_width)
        weighted = (block_values[:, None, :] * hot_low[None]).reshape(fields * low_width, length)
        summed = lax.dot_general(
            weighted, hot_high, (((1,), (1,)), ((), ())), precision=lax.Precision.HIGHEST
        )
        return (running + summed, None)

    start = jnp.zeros((fields * low_width, high_width), jnp.float32)
    running, unused = lax.scan(add_block, start, (flat_ids.reshape(blocks, length), value_blocks))
    return (
        running.reshape(fields, low_width, high_width).transpose(0, 2, 1).reshape(fields, cameras)
    )


def predict(camera_field, cam_jac, obs_camera):
    at_obs = gather_cameras(camera_field, obs_camera)
    return jnp.sum(cam_jac * at_obs[None], axis=1)


def schur_terms(camera_field, cam_jac, point_jac, obs_camera, inverse, cameras):
    predicted = predict(camera_field, cam_jac, obs_camera)
    pulled = jnp.sum(point_jac * predicted[:, None], axis=(0, 2))
    solved = jnp.sum(inverse * pulled[None], axis=1)
    remain = predicted - jnp.sum(point_jac * solved[None, :, None], axis=1)
    return scatter_cameras(jnp.sum(cam_jac * remain[:, None], axis=0), obs_camera, cameras)


def body(cam_jac, point_jac, residuals, obs_camera, damping):
    damp_value = damping[0]
    cameras = NCAM
    params = cam_jac.shape[1]
    inverse = point_inverse(point_jac, damp_value)
    grad_point = jnp.sum(point_jac * residuals[:, None], axis=(0, 2))
    lifted = jnp.sum(inverse * grad_point[None], axis=1)
    remain = residuals - jnp.sum(point_jac * lifted[None, :, None], axis=1)
    stacked = jnp.concatenate(
        [jnp.sum(cam_jac * remain[:, None], axis=0), jnp.sum(cam_jac * cam_jac, axis=0)], axis=0
    )
    both_terms = scatter_cameras(stacked, obs_camera, cameras)
    right_terms = -both_terms[:params]
    diagonal_terms = both_terms[params:]
    right_side, diagonal = lax.psum((right_terms, diagonal_terms), "pts")
    precond = damp_value + diagonal
    solution = jnp.zeros_like(right_side)
    residual_vec = right_side
    scaled = residual_vec / precond
    direction = scaled
    norm_now = jnp.sum(residual_vec * scaled)
    for iteration in range(ITERS):
        summed = lax.psum(
            schur_terms(direction, cam_jac, point_jac, obs_camera, inverse, cameras), "pts"
        )
        image = damp_value * direction + summed
        step_size = norm_now / jnp.sum(direction * image)
        solution = solution + step_size * direction
        residual_vec = residual_vec - step_size * image
        if iteration + 1 < ITERS:
            scaled = residual_vec / precond
            norm_next = jnp.sum(residual_vec * scaled)
            direction = scaled + norm_next / norm_now * direction
            norm_now = norm_next
    per_device = cameras // lax.axis_size("pts")
    offset = lax.axis_index("pts") * per_device
    camera_step = lax.dynamic_slice_in_dim(solution, offset, per_device, 1)
    predicted = predict(solution, cam_jac, obs_camera)
    pulled = grad_point + jnp.sum(point_jac * predicted[:, None], axis=(0, 2))
    point_step = -jnp.sum(inverse * pulled[None], axis=1)
    return (camera_step, point_step)


def solution(mesh):
    in_specs = (
        P(None, None, None, ("sub", "pts")),
        P(None, None, None, ("sub", "pts")),
        P(None, None, ("sub", "pts")),
        P(None, ("sub", "pts")),
        P("sub"),
    )
    out_specs = (P(None, ("sub", "pts")), P(None, ("sub", "pts")))
    return jax.shard_map(body, mesh=mesh, in_specs=in_specs, out_specs=out_specs, check_vma=False)
```

profile of v0, /device:TPU:0, one launch (start us, length us, event | category | flops | bytes accessed | tf_op | source)
XLA Modules:
  0.0 602.2 jit_solution(17663560836401889620)
XLA Ops:
  7.9 1.1 multiply_reduce_fusion.13
  13.0 6.3 %while.104 = (s32[]{:T(128)}, f32[288,256]{1,0:T(8,128)S(1)}, f32[8,18,512]{2,0,1:T(8,128)S(1)}, s32[8,512]{1,0:T(8,128)S(1)}, s32[]{:T(128)}, /*index=5*/s32[]{:T(128)}) while((s32[]{:T(128)}, f32[288,256]{1,0:T(8,128)S(1)}, f32[8,18,512]{2,0,1:T(8,128)S(1)}, s32[8,512]{1,0:T(8,128)S(1)}, s32[]{:T(128)}, ...), condition=%wide.region_7.8_spmd.clone, body=%wide.region_6.7_spmd.clone.sunk | while | flops 453437440 | bytes 2033751 | solution.py:93
  20.0 1.6 fusion.21
  21.6 2.8 neg.10
  24.4 1.4 slice.37
  25.9 132.2 %all-reduce.12.cloned.1.call-done = (f32[9,4096]{1,0:T(8,128)}, f32[9,4096]{1,0:T(8,128)}) async-done(((f32[9,4096]{1,0:T(8,128)}, f32[9,4096]{1,0:T(8,128)}), (f32[9,4096]{1,0:T(8,128)}, f32[9,4096]{1,0:T(8,128)})) %all-reduce.12.cloned.1.call-update) | async-done | bytes 294928 | tf_op jit(solution)/shard_map/psum | solution.py:126
  159.9 4.0 while.100
  165.1 5.0 while.105
  170.5 1.4 reshape.764
  172.0 125.7 %all-reduce.6.cloned.1.call-done = f32[9,4096]{1,0:T(8,128)} async-done(((f32[9,4096]{1,0:T(8,128)}), f32[9,4096]{1,0:T(8,128)}) %all-reduce.6.cloned.1.call-update) | async-done | bytes 147472 | tf_op jit(solution)/shard_map/psum | solution.py:134
  297.7 1.7 multiply_reduce_fusion.18
  300.6 1.7 multiply_reduce_fusion.17
  304.4 4.0 while.101
  309.0 5.0 while.106
  314.4 1.4 reshape.769
  316.0 125.6 %all-reduce.8.cloned.1.call-done = f32[9,4096]{1,0:T(8,128)} async-done(((f32[9,4096]{1,0:T(8,128)}), f32[9,4096]{1,0:T(8,128)}) %all-reduce.8.cloned.1.call-update) | async-done | bytes 147472 | tf_op jit(solution)/shard_map/psum | solution.py:134
  441.6 1.7 multiply_reduce_fusion.16
  444.6 1.7 multiply_reduce_fusion.15
  448.6 4.0 while.102
  453.2 5.0 while.107
  458.6 1.4 reshape.774
  460.0 125.8 %all-reduce.10.cloned.1.call-done = f32[9,4096]{1,0:T(8,128)} async-done(((f32[9,4096]{1,0:T(8,128)}), f32[9,4096]{1,0:T(8,128)}) %all-reduce.10.cloned.1.call-update) | async-done | bytes 147472 | tf_op jit(solution)/shard_map/psum | solution.py:134
  585.8 1.7 multiply_reduce_fusion.14
  589.7 4.0 while.103
  (517 shorter events, 47.8 us)
Async XLA Ops:
  7.2 5.4 copy-start
  7.2 150.9 %all-reduce.12.cloned.1.call-start = ((), (), s32[]{:S(2)}) async-start(), calls=%async_computation.3 | async-start | bytes 1048576 | tf_op jit(solution)/shard_map/psum | solution.py:126
  10.1 2.6 copy-start.7
  10.2 2.8 copy-start.9
  21.6 2.8 copy-start.3
  25.8 271.9 %all-reduce.6.cloned.1.call-start = ((), (), s32[]{:S(2)}) async-start(), calls=%async_computation | async-start | bytes 524288 | tf_op jit(solution)/shard_map/psum | solution.py:134
  163.9 0.9 copy-start.1
  163.9 0.9 copy-start.6
  170.5 127.2 %copy-start.5 = (f32[9,4096]{1,0:T(8,128)S(1)}, f32[9,4096]{1,0:T(8,128)}, u32[]{:S(2)}) copy-start(f32[9,4096]{1,0:T(8,128)} %get-tuple-element.634) | copy-start | bytes 442372
  170.5 130.1 %copy-start.2 = (f32[9,4096]{1,0:T(8,128)S(1)}, f32[9,4096]{1,0:T(8,128)}, u32[]{:S(2)}) copy-start(f32[9,4096]{1,0:T(8,128)} %get-tuple-element.635) | copy-start | bytes 442372
  172.0 269.6 %all-reduce.8.cloned.1.call-start = ((), (), s32[]{:S(2)}) async-start(), calls=%async_computation.1 | async-start | bytes 524288 | tf_op jit(solution)/shard_map/psum | solution.py:134
  315.8 270.0 %all-reduce.10.cloned.1.call-start = ((), (), s32[]{:S(2)}) async-start(), calls=%async_computation.2 | async-start | bytes 524288 | tf_op jit(solution)/shard_map/psum | solution.py:134
  441.6 6.1 %copy-start.4 = (f32[9,4096]{1,0:T(8,128)S(1)}, f32[9,4096]{1,0:T(8,128)}, u32[]{:S(2)}) copy-start(f32[9,4096]{1,0:T(8,128)} %all-reduce.8.cloned.1.call-done) | copy-start | bytes 442372
  593.7 0.7 copy-start.8
Sparse Core Ops, SparseCore 0:
  25.9 132.0 all-reduce.11
  172.1 125.5 all-reduce.5
  315.9 125.6 all-reduce.7
  460.1 125.6 all-reduce.9
where the time goes:
time: 603 us; the launch traced here: 602 us
  waiting for transfers between devices  509 us (84%)
  matrix products  26.7 us (4%)
  other arithmetic  23.2 us (4%)
  between operations  21.5 us (4%)
  local copies, waits for them, and re-layouts  17.1 us (3%)
    psum x3, waiting for transfers between devices, body(): lax.psum(schur_terms(direction, cam_jac, point_jac, obs_camera, inverse,...  377 us
    psum x1, waiting for transfers between devices, body(): right_side, diagonal = lax.psum((right_terms, diagonal_terms), 'pts')  132 us
    dot_general x32, matrix products, add_block(): lax.dot_general(weighted, hot_high, (((1,), (1,)), ((), ())), precision=l...  16 us
  transfers between devices with their start and end apart: 4, of which 4 were waited for; matrix products, arithmetic and copies ran while one was open for 0% of the time, Pallas kernels for 0%

commit v1 on v0

--- a/solution.py
+++ b/solution.py
@@ -131,8 +131,11 @@
     direction = scaled
     norm_now = jnp.sum(residual_vec * scaled)
     for iteration in range(ITERS):
-        summed = lax.psum(
-            schur_terms(direction, cam_jac, point_jac, obs_camera, inverse, cameras), "pts"
+        summed = jnp.sum(
+            lax.all_gather(
+                schur_terms(direction, cam_jac, point_jac, obs_camera, inverse, cameras), "pts"
+            ),
+            axis=0,
         )
         image = damp_value * direction + summed
         step_size = norm_now / jnp.sum(direction * image)

time: 603 us -> 459 us (0.76)
  waiting for transfers between devices: 509 us -> 360 us
  other arithmetic: 23.2 us -> 29.3 us
    psum x3 -> x0, waiting for transfers between devices: 377 us -> none  [body(): lax.psum(schur_terms(direction, cam_jac, point_jac, obs_camera, inverse,...]
    all_gather x0 -> x3, waiting for transfers between devices: none -> 228 us  [body(): lax.all_gather(schur_terms(direction, cam_jac, point_jac, obs_camera, inv...]
    reduce_sum x0 -> x3, other arithmetic: none -> 11.7 us  [body(): jnp.sum(lax.all_gather(schur_terms(direction, cam_jac, point_jac, obs_cam...]
where the time goes in v1:
time: 459 us; the launch traced here: 458 us
  waiting for transfers between devices  360 us (78%)
  other arithmetic  29.3 us (6%)
  matrix products  26.7 us (6%)
  between operations  21.5 us (5%)
  local copies, waits for them, and re-layouts  16.7 us (4%)
    all_gather x3, waiting for transfers between devices, body(): lax.all_gather(schur_terms(direction, cam_jac, point_jac, obs_camera, inv...  228 us
    psum x1, waiting for transfers between devices, body(): right_side, diagonal = lax.psum((right_terms, diagonal_terms), 'pts')  132 us
    dot_general x32, matrix products, add_block(): lax.dot_general(weighted, hot_high, (((1,), (1,)), ((), ())), precision=l...  16 us
    reduce_sum x3, other arithmetic, body(): jnp.sum(lax.all_gather(schur_terms(direction, cam_jac, point_jac, obs_cam...  11.7 us
    dot_general x32, matrix products, one_block(): jnp.dot(lookup, hot_high, precision=lax.Precision.HIGHEST)  10.7 us
  transfers between devices with their start and end apart: 4, of which 4 were waited for; matrix products, arithmetic and copies ran while one was open for 0% of the time, Pallas kernels for 0%

profile of v1, /device:TPU:0, one launch (start us, length us, event | category | flops | bytes accessed | tf_op | source)
XLA Modules:
  0.0 458.4 jit_solution(3396863518544258326)
XLA Ops:
  7.9 1.1 multiply_reduce_fusion.13
  9.2 0.9 multiply_reduce_fusion.28
  12.4 6.3 %while.104 = (s32[]{:T(128)}, f32[288,256]{1,0:T(8,128)S(1)}, f32[8,18,512]{2,0,1:T(8,128)S(1)}, s32[8,512]{1,0:T(8,128)S(1)}, s32[]{:T(128)}, /*index=5*/s32[]{:T(128)}) while((s32[]{:T(128)}, f32[288,256]{1,0:T(8,128)S(1)}, f32[8,18,512]{2,0,1:T(8,128)S(1)}, s32[8,512]{1,0:T(8,128)S(1)}, s32[]{:T(128)}, ...), condition=%wide.region_7.8_spmd.clone, body=%wide.region_6.7_spmd.clone.sunk | while | flops 453437440 | bytes 2033751 | solution.py:93
  19.4 1.6 fusion.21
  21.0 2.8 neg.10
  23.8 1.4 slice.37
  25.3 132.2 %all-reduce.3.cloned.1.call-done = (f32[9,4096]{1,0:T(8,128)}, f32[9,4096]{1,0:T(8,128)}) async-done(((f32[9,4096]{1,0:T(8,128)}, f32[9,4096]{1,0:T(8,128)}), (f32[9,4096]{1,0:T(8,128)}, f32[9,4096]{1,0:T(8,128)})) %all-reduce.3.cloned.1.call-update) | async-done | bytes 294928 | tf_op jit(solution)/shard_map/psum | solution.py:126
  157.4 1.1 add_divide_fusion.2
  159.3 4.0 while.100
  164.5 5.0 %while.105 = (s32[]{:T(128)}, f32[144,256]{1,0:T(8,128)S(1)}, f32[8,9,512]{2,0,1:T(8,128)S(1)}, s32[8,512]{1,0:T(8,128)S(1)}, s32[]{:T(128)}, /*index=5*/s32[]{:T(128)}) while((s32[]{:T(128)}, f32[144,256]{1,0:T(8,128)S(1)}, f32[8,9,512]{2,0,1:T(8,128)S(1)}, s32[8,512]{1,0:T(8,128)S(1)}, s32[]{:T(128)}, ...), condition=%wide.region_20.21_spmd.clone, body=%wide.region_19.20_spmd.clone.sunk | while | flops 226797568 | bytes 1056855 | solution.py:93
  169.9 1.4 all_gather_reshape.9
  171.4 76.1 %all-gather.4.cloned.1.call-done = f32[32,9,4096]{2,1,0:T(8,128)} async-done(((f32[1,9,4096]{2,1,0:T(8,128)}), f32[32,9,4096]{2,1,0:T(8,128)}) %all-gather.4.cloned.1.call-update) | async-done | bytes 4718608 | tf_op jit(solution)/shard_map/all_gather | solution.py:135
  247.6 3.9 reduce_sum.357
  256.4 4.0 while.101
  261.0 5.0 %while.106 = (s32[]{:T(128)}, f32[144,256]{1,0:T(8,128)S(1)}, f32[8,9,512]{2,0,1:T(8,128)S(1)}, s32[8,512]{1,0:T(8,128)S(1)}, s32[]{:T(128)}, /*index=5*/s32[]{:T(128)}) while((s32[]{:T(128)}, f32[144,256]{1,0:T(8,128)S(1)}, f32[8,9,512]{2,0,1:T(8,128)S(1)}, s32[8,512]{1,0:T(8,128)S(1)}, s32[]{:T(128)}, ...), condition=%wide.region_33.34_spmd.clone, body=%wide.region_32.33_spmd.clone.sunk | while | flops 226797568 | bytes 1056855 | solution.py:93
  266.3 1.4 all_gather_reshape.10
  268.0 75.6 %all-gather.6.cloned.1.call-done = f32[32,9,4096]{2,1,0:T(8,128)} async-done(((f32[1,9,4096]{2,1,0:T(8,128)}), f32[32,9,4096]{2,1,0:T(8,128)}) %all-gather.6.cloned.1.call-update) | async-done | bytes 4718608 | tf_op jit(solution)/shard_map/all_gather | solution.py:135
  343.6 3.9 reduce_sum.365
  352.3 4.0 while.102
  356.9 5.0 %while.107 = (s32[]{:T(128)}, f32[144,256]{1,0:T(8,128)S(1)}, f32[8,9,512]{2,0,1:T(8,128)S(1)}, s32[8,512]{1,0:T(8,128)S(1)}, s32[]{:T(128)}, /*index=5*/s32[]{:T(128)}) while((s32[]{:T(128)}, f32[144,256]{1,0:T(8,128)S(1)}, f32[8,9,512]{2,0,1:T(8,128)S(1)}, s32[8,512]{1,0:T(8,128)S(1)}, s32[]{:T(128)}, ...), condition=%wide.region_46.47_spmd.clone, body=%wide.region_45.46_spmd.clone.sunk | while | flops 226797568 | bytes 1056855 | solution.py:93
  362.3 1.4 all_gather_reshape.11
  363.7 75.8 %all-gather.8.cloned.1.call-done = f32[32,9,4096]{2,1,0:T(8,128)} async-done(((f32[1,9,4096]{2,1,0:T(8,128)}), f32[32,9,4096]{2,1,0:T(8,128)}) %all-gather.8.cloned.1.call-update) | async-done | bytes 4718608 | tf_op jit(solution)/shard_map/all_gather | solution.py:135
  439.5 3.9 reduce_sum.373
  446.3 4.0 while.103
  (512 shorter events, 48.2 us)
Async XLA Ops:
  7.2 4.8 %copy-start = (f32[2,9,4,1024]{3,2,1,0:T(4,128)S(1)}, f32[2,9,4,1024]{3,2,1,0:T(4,128)}, u32[]{:S(2)}) copy-start(f32[2,9,4,1024]{3,2,1,0:T(4,128)} %param.21) | copy-start | bytes 884740
  7.2 150.3 %all-reduce.3.cloned.1.call-start = ((), (), s32[]{:S(2)}) async-start(), calls=%async_computation.3 | async-start | bytes 1048576 | tf_op jit(solution)/shard_map/psum | solution.py:126
  10.1 2.2 copy-start.5
  21.0 2.8 copy-start.3
  25.2 222.3 %all-gather.4.cloned.1.call-start = ((), (), s32[]{:S(2)}) async-start(), calls=%async_computation | async-start | bytes 8650752 | tf_op jit(solution)/shard_map/all_gather | solution.py:135
  163.3 0.9 copy-start.1
  171.4 172.3 %all-gather.6.cloned.1.call-start = ((), (), s32[]{:S(2)}) async-start(), calls=%async_computation.1 | async-start | bytes 8650752 | tf_op jit(solution)/shard_map/all_gather | solution.py:135
  171.4 80.1 %copy-start.4 = (f32[9,4096]{1,0:T(8,128)S(1)}, f32[9,4096]{1,0:T(8,128)}, u32[]{:S(2)}) copy-start(f32[9,4096]{1,0:T(8,128)} %get-tuple-element.650) | copy-start | bytes 442372
  171.4 82.1 %copy-start.2 = (f32[9,4096]{1,0:T(8,128)S(1)}, f32[9,4096]{1,0:T(8,128)}, u32[]{:S(2)}) copy-start(f32[9,4096]{1,0:T(8,128)} %get-tuple-element.651) | copy-start | bytes 442372
  267.8 171.7 %all-gather.8.cloned.1.call-start = ((), (), s32[]{:S(2)}) async-start(), calls=%async_computation.2 | async-start | bytes 8650752 | tf_op jit(solution)/shard_map/all_gather | solution.py:135
Sparse Core Ops, SparseCore 0:
  25.3 132.0 all-reduce.2
  171.5 76.0 all-gather.3
  267.9 75.6 all-gather.5
  363.8 75.6 all-gather.7
